TPU v7x, 512 devices: a whole 4x8x8 slice. The times are simulated.
512 devices in a mesh: af: 16 (over z, core), gy: 4 (over x), gz: 8 (over y).
Axes of the slice: x: 4, y: 8, z: 8, core: 2. Of those that a mesh axis runs over, the one named last changes fastest.
Arguments:
- slab: bfloat16 [512, 262144], P('af', ('gy', 'gz')), may hold values from -4000 to 4000
- block_owner: int32 [4, 8, 16], P('gy', 'gz'), may hold values from 0 to 15, each once within a row
- basis_init: float32 [512, 128], replicated, may hold values from -0.25 to 0.25
Outputs:
- triangle: float32 [512, 512], replicated
- basis: float32 [512, 128], replicated
- core: bfloat16 [128, 262144], P(None, ('gy', 'gz', 'af'))
Inputs may be any that keep to these rules, and one draw needn't show every extreme that they name: For every gy and gz index, block_owner[gy, gz, :] is a permutation of the 16 af indices.
All inputs are finite; a program needn't handle non-finite values.
Results may differ from a plain program's by a relative error of at most 0.0049.
Values may be sent and summed in bfloat16 or wider, within the bound.
A program may use at most 64 MiB of HBM per device.

v0:
```python
import functools
import jax
import jax.numpy as jnp
from jax import lax
from jax.experimental import pallas as pl
from jax.experimental.pallas import tpu as pltpu
from jax.sharding import PartitionSpec as P

TILE = 128
STRIP = 8
exact_mode = lax.Precision.HIGHEST
MESH = pl.DeviceIdType.MESH


def ring_offsets(size):
    return sorted(range(1, size), key=lambda step: -min(step, size - step))


def exchange_kernel(
    sizes, outgoing, columns_ref, gram_ref,
    part, pair_land, pair_sum, x_land, x_sum, y_land, z_land, y_gather, x_gather,
    a2a_send, a2a_recv, pair_send, pair_recv, x_send, x_recv, y_send, y_recv, z_send, z_recv,
    yg_send, yg_recv, xg_send, xg_recv, final_send, final_recv,
):
    fibers, x_size, y_size = sizes
    z_size = fibers // 2
    rows, block_cols = outgoing.shape[1:]
    fiber = lax.axis_index("af")
    x = lax.axis_index("gy")
    y = lax.axis_index("gz")
    z, core = fiber // 2, fiber % 2
    half = pair_sum.shape[0]
    x_rows = x_sum.shape[0]
    y_rows = y_land.shape[1]

    def fiber_at(z_step, core_step):
        return ((z + z_step) % z_size) * 2 + (core + core_step) % 2

    fiber_steps = [(s, c) for s in ring_offsets(z_size) for c in (0, 1)] + [(0, 1)]
    barrier = pltpu.get_barrier_semaphore()
    for z_step, core_step in fiber_steps:
        pl.semaphore_signal(barrier, inc=1, device_id={"af": fiber_at(z_step, core_step)}, device_id_type=MESH)
    for step in range(1, y_size):
        pl.semaphore_signal(barrier, inc=1, device_id={"gz": (y + step) % y_size}, device_id_type=MESH)
    for step in range(1, x_size):
        pl.semaphore_signal(barrier, inc=1, device_id={"gy": (x + step) % x_size}, device_id_type=MESH)

    pl.semaphore_wait(barrier, len(fiber_steps) + x_size + y_size - 2)

    my_rows = pl.ds(pl.multiple_of(fiber * rows, rows), rows)
    copies = []
    for index, (z_step, core_step) in enumerate(fiber_steps):
        peer = fiber_at(z_step, core_step)
        copy = pltpu.make_async_remote_copy(
            src_ref=outgoing.at[peer], dst_ref=columns_ref.at[my_rows],
            send_sem=a2a_send.at[index], recv_sem=a2a_recv.at[index],
            device_id={"af": peer}, device_id_type=MESH,
        )
        copy.start()
        copies.append(copy)
    columns_ref[my_rows, :] = outgoing[fiber]
    for copy in copies:
        copy.wait()

    scale = 1.0 / (block_cols * fibers * x_size * y_size)
    pairs = [(i, j) for i in range(4) for j in range(i + 1)]
    per_core = len(pairs) // 2

    def gram_blocks(owner):
        for index in range(per_core):
            (i0, j0), (i1, j1) = pairs[index], pairs[per_core + index]
            i = i0 + owner * (i1 - i0)
            j = j0 + owner * (j1 - j0)
            left = columns_ref[pl.ds(pl.multiple_of(i * TILE, TILE), TILE), :]
            right = columns_ref[pl.ds(pl.multiple_of(j * TILE, TILE), TILE), :]
            product = lax.dot_general(left, right, (((1,), (1,)), ((), ())), preferred_element_type=jnp.float32)
            at = pl.multiple_of(owner * half + index * TILE, TILE)
            part[pl.ds(at, TILE), :] = product * scale

    other = (core + 1) % 2
    gram_blocks(other)
    pair = pltpu.make_async_remote_copy(
        src_ref=part.at[pl.ds(pl.multiple_of(other * half, half), half)], dst_ref=pair_land,
        send_sem=pair_send, recv_sem=pair_recv,
        device_id={"af": fiber_at(0, 1)}, device_id_type=MESH,
    )
    pair.start()
    gram_blocks(core)
    pair.wait()
    my_half = pl.ds(pl.multiple_of(core * half, half), half)
    pair_sum[...] = part[my_half, :] + pair_land[...]

    copies = []
    for step in ring_offsets(x_size):
        peer = (x + step) % x_size
        copy = pltpu.make_async_remote_copy(
            src_ref=pair_sum.at[pl.ds(pl.multiple_of(peer * x_rows, x_rows), x_rows)], dst_ref=x_land.at[step - 1],
            send_sem=x_send.at[step - 1], recv_sem=x_recv.at[step - 1],
            device_id={"gy": peer}, device_id_type=MESH,
        )
        copy.start()
        copies.append(copy)
    for copy in copies:
        copy.wait()
    total = pair_sum[pl.ds(pl.multiple_of(x * x_rows, x_rows), x_rows), :]
    for step in range(1, x_size):
        total = total + x_land[step - 1]
    x_sum[...] = total

    def tile_start(owner):
        return (owner * (x_rows // 8) // y_size) * 8

    copies = []
    for step in ring_offsets(y_size):
        peer = (y + step) % y_size
        copy = pltpu.make_async_remote_copy(
            src_ref=x_sum.at[pl.ds(pl.multiple_of(tile_start(peer), 8), y_rows)], dst_ref=y_land.at[step - 1],
            send_sem=y_send.at[step - 1], recv_sem=y_recv.at[step - 1],
            device_id={"gz": peer}, device_id_type=MESH,
        )
        copy.start()
        copies.append(copy)
    for copy in copies:
        copy.wait()
    total = x_sum[pl.ds(pl.multiple_of(tile_start(y), 8), y_rows), :]
    for step in range(1, y_size):
        total = total + y_land[step - 1]

    z_land[z] = total
    copies = []
    for step in ring_offsets(z_size):
        peer = fiber_at(step, 0)
        copy = pltpu.make_async_remote_copy(
            src_ref=z_land.at[z], dst_ref=z_land.at[z],
            send_sem=z_send.at[step - 1], recv_sem=z_recv.at[step - 1],
            device_id={"af": peer}, device_id_type=MESH,
        )
        copy.start()
        copies.append(copy)
    for copy in copies:
        copy.wait()
    total = z_land[0]
    for index in range(1, z_size):
        total = total + z_land[index]

    y_gather[y] = total
    copies = []
    for step in ring_offsets(y_size):
        peer = (y + step) % y_size
        copy = pltpu.make_async_remote_copy(
            src_ref=y_gather.at[y], dst_ref=y_gather.at[y],
            send_sem=yg_send.at[step - 1], recv_sem=yg_recv.at[step - 1],
            device_id={"gz": peer}, device_id_type=MESH,
        )
        copy.start()
        copies.append(copy)
    for copy in copies:
        copy.wait()
    my_x = pl.multiple_of(x * x_rows, x_rows)
    for owner in range(y_size):
        first = tile_start(owner)
        last = tile_start(owner + 1) if owner + 1 < y_size else x_rows
        x_gather[pl.ds(pl.multiple_of(my_x + first, 8), last - first), :] = y_gather[owner, : last - first, :]

    copies = []
    mine = pl.ds(my_x, x_rows)
    for step in ring_offsets(x_size):
        peer = (x + step) % x_size
        copy = pltpu.make_async_remote_copy(
            src_ref=x_gather.at[mine], dst_ref=x_gather.at[mine],
            send_sem=xg_send.at[step - 1], recv_sem=xg_recv.at[step - 1],
            device_id={"gy": peer}, device_id_type=MESH,
        )
        copy.start()
        copies.append(copy)
    for copy in copies:
        copy.wait()

    final = pltpu.make_async_remote_copy(
        src_ref=x_gather, dst_ref=gram_ref.at[my_half],
        send_sem=final_send, recv_sem=final_recv,
        device_id={"af": fiber_at(0, 1)}, device_id_type=MESH,
    )
    final.start()
    gram_ref[my_half, :] = x_gather[...]
    final.wait()


def exchange(arranged):
    sizes = (lax.axis_size("af"), lax.axis_size("gy"), lax.axis_size("gz"))
    fibers, x_size, y_size = sizes
    z_size = fibers // 2
    rows, block_cols = arranged.shape[1:]
    all_rows = rows * fibers
    half = 5 * TILE
    x_rows = half // x_size
    y_rows = max(
        (((p + 1) * (x_rows // 8)) // y_size - (p * (x_rows // 8)) // y_size) for p in range(y_size)
    ) * 8
    dma = pltpu.SemaphoreType.DMA
    f32, bf16 = jnp.float32, jnp.bfloat16
    return pl.pallas_call(
        functools.partial(exchange_kernel, sizes),
        out_shape=(
            jax.ShapeDtypeStruct((all_rows, block_cols), bf16),
            jax.ShapeDtypeStruct((2 * half, TILE), f32),
        ),
        in_specs=[pl.BlockSpec(memory_space=pltpu.VMEM)],
        out_specs=[pl.BlockSpec(memory_space=pltpu.VMEM)] * 2,
        scratch_shapes=[
            pltpu.VMEM((2 * half, TILE), f32),
            pltpu.VMEM((half, TILE), f32),
            pltpu.VMEM((half, TILE), f32),
            pltpu.VMEM((x_size - 1, x_rows, TILE), f32),
            pltpu.VMEM((x_rows, TILE), f32),
            pltpu.VMEM((y_size - 1, y_rows, TILE), f32),
            pltpu.VMEM((z_size, y_rows, TILE), f32),
            pltpu.VMEM((y_size, y_rows, TILE), f32),
            pltpu.VMEM((half, TILE), f32),
            dma((fibers - 1,)), dma((fibers - 1,)), dma, dma,
            dma((x_size - 1,)), dma((x_size - 1,)), dma((y_size - 1,)), dma((y_size - 1,)),
            dma((z_size - 1,)), dma((z_size - 1,)),
            dma((y_size - 1,)), dma((y_size - 1,)), dma((x_size - 1,)), dma((x_size - 1,)), dma, dma,
        ],
        compiler_params=pltpu.CompilerParams(collective_id=0, has_side_effects=True, vmem_limit_bytes=32 << 20),
    )(arranged)


def eliminate_strip(work, final, scales, first):
    f32 = jnp.float32
    shape = (STRIP, TILE)
    lane = lax.broadcasted_iota(jnp.int32, shape, 1)
    sub = lax.broadcasted_iota(jnp.int32, shape, 0)
    strip = work[pl.ds(first, STRIP), :]
    rolled = pltpu.roll(strip, TILE - first, 1)
    heads = [jnp.broadcast_to(rolled[:, t : t + 1], shape) for t in range(STRIP)]
    full = strip
    down = strip
    scale = jnp.zeros(shape, f32)
    for t in range(STRIP):
        head = heads[t]
        pivot = jnp.broadcast_to(head[t : t + 1, :], shape)
        inverse = 1.0 / pivot
        scale = jnp.where(sub == t, lax.rsqrt(pivot), scale)
        factor = head * inverse
        here = lane == first + t
        row = jnp.where(here, 1.0, jnp.broadcast_to(full[t : t + 1, :], shape))
        full = jnp.where(sub == t, row * inverse, jnp.where(here, 0.0, full) - factor * row)
        drow = jnp.where(here, 1.0, jnp.broadcast_to(down[t : t + 1, :], shape))
        down = jnp.where(sub > t, jnp.where(here, 0.0, down) - factor * drow, down)
        for u in range(t + 1, STRIP):
            line = jnp.broadcast_to(heads[u][t : t + 1, :], shape)
            heads[u] = jnp.where(sub == t, line * inverse, heads[u] - factor * line)
    final[pl.ds(first, STRIP), :] = down * scale
    scales[pl.ds(first, STRIP), :] = scale
    return full


def strip_update(work, full, first):
    lane = lax.broadcasted_iota(jnp.int32, (TILE, TILE), 1)
    sub = lax.broadcasted_iota(jnp.int32, (TILE, TILE), 0)
    rows = work[...]
    own = (lane >= first) & (lane < first + STRIP)
    below = sub >= first + STRIP
    head = pltpu.roll(rows, TILE - first, 1)[:, :STRIP]
    update = jnp.dot(head, full, precision=exact_mode, preferred_element_type=jnp.float32)
    work[...] = jnp.where(below, jnp.where(own, 0.0, rows) - update, rows)


def factor_both(works, finals, scales):
    @pl.loop(0, TILE // STRIP)
    def _(index):
        first = pl.multiple_of(index * STRIP, STRIP)
        fulls = [eliminate_strip(w, f, s, first) for w, f, s in zip(works, finals, scales)]
        for work, full in zip(works, fulls):
            strip_update(work, full, first)


def inverse_of(final, scales):
    lane = lax.broadcasted_iota(jnp.int32, (TILE, TILE), 1)
    sub = lax.broadcasted_iota(jnp.int32, (TILE, TILE), 0)
    return jnp.where(lane < sub, final[...], jnp.where(lane == sub, scales[...], 0.0))


def upper_of(final):
    lane = lax.broadcasted_iota(jnp.int32, (TILE, TILE), 1)
    sub = lax.broadcasted_iota(jnp.int32, (TILE, TILE), 0)
    return jnp.where(lane >= sub, final[...], 0.0)


def dot_exact(a, b, dims):
    return lax.dot_general(a, b, (dims, ((), ())), precision=exact_mode, preferred_element_type=jnp.float32)


NN, NT, TN = ((1,), (0,)), ((1,), (1,)), ((0,), (0,))


def factor_kernel(
    packed_ref, start_ref, columns_ref, triangle_ref, basis_ref, core_ref,
    gram, trail, product, work_a, work_b, final_a, final_b, scale_a, scale_b,
):
    count = 4
    spot = lambda i, j: pl.ds((i * (i + 1) // 2 + j) * TILE, TILE)
    at = lambda i: pl.ds(i * TILE, TILE)
    for i in range(count):
        for j in range(i + 1):
            block = packed_ref[spot(i, j), :]
            gram[at(i), at(j)] = block
            trail[at(i), at(j)] = block
            if i != j:
                gram[at(j), at(i)] = block.T
                triangle_ref[at(j), at(i)] = jnp.zeros((TILE, TILE), jnp.float32)
    start = start_ref[...]
    image = dot_exact(gram[...], start, NN)
    product[...] = image
    work_b[...] = dot_exact(start, image, TN)
    for k in range(count):
        work_a[...] = trail[at(k), at(k)]
        factor_both((work_a, work_b), (final_a, final_b), (scale_a, scale_b))
        turn = inverse_of(final_b, scale_b)
        image = dot_exact(product[...], turn, NT)
        if k == 0 or k == 2:
            product[...] = image
            work_b[...] = dot_exact(image, image, TN)
        elif k == 1:
            moved = dot_exact(gram[...], image, NN)
            product[...] = moved
            work_b[...] = dot_exact(image, moved, TN)
        else:
            basis_ref[...] = image
            core_ref[...] = lax.dot_general(
                image.astype(jnp.bfloat16), columns_ref[...], (TN, ((), ())), preferred_element_type=jnp.float32
            ).astype(jnp.bfloat16)
        triangle_ref[at(k), at(k)] = upper_of(final_a).T
        if k + 1 < count:
            rest = pl.ds((k + 1) * TILE, (count - 1 - k) * TILE)
            lower = dot_exact(trail[rest, at(k)], inverse_of(final_a, scale_a), NT)
            triangle_ref[rest, at(k)] = lower
            for j in range(k + 1, count):
                tail = pl.ds(j * TILE, (count - j) * TILE)
                skip = (j - k - 1) * TILE
                trail[tail, at(j)] = trail[tail, at(j)] - dot_exact(lower[skip:], lower[skip : skip + TILE], NT)


def factor(packed, start, columns):
    f32 = jnp.float32
    rows, rank = start.shape
    square = pltpu.VMEM((TILE, TILE), f32)
    return pl.pallas_call(
        factor_kernel,
        out_shape=(
            jax.ShapeDtypeStruct((rows, rows), f32),
            jax.ShapeDtypeStruct((rows, rank), f32),
            jax.ShapeDtypeStruct((rank, columns.shape[1]), jnp.bfloat16),
        ),
        in_specs=[pl.BlockSpec(memory_space=pltpu.VMEM)] * 3,
        out_specs=[pl.BlockSpec(memory_space=pltpu.VMEM)] * 3,
        scratch_shapes=[
            pltpu.VMEM((rows, rows), f32), pltpu.VMEM((rows, rows), f32), pltpu.VMEM((rows, rank), f32),
            square, square, square, square, square, square,
        ],
        compiler_params=pltpu.CompilerParams(vmem_limit_bytes=32 << 20),
    )(packed, start, columns)


def on_device(slab, block_owner, basis_init):
    fibers = lax.axis_size("af")
    labels = jnp.arange(fibers, dtype=jnp.int32)
    onehot = (block_owner.reshape(fibers)[:, None] == labels[None, :]).astype(jnp.int32)
    source = jnp.sum(onehot * labels[:, None], axis=0)
    pieces = slab.reshape(slab.shape[0], fibers, -1)
    columns, packed = exchange(jnp.take(pieces, source, axis=1).transpose(1, 0, 2))
    return factor(packed, basis_init, columns)


def solution(mesh):
    placed = (P("af", ("gy", "gz")), P("gy", "gz", None), P())
    return jax.shard_map(
        on_device,
        mesh=mesh,
        in_specs=placed,
        out_specs=(P(), P(), P(None, ("gy", "gz", "af"))),
        check_vma=False,
    )
```

profile of v0, /device:TPU:1, one launch (start us, length us, event | category | flops | bytes accessed | tf_op | source)
XLA Modules:
  0.0 103.5 jit_solution(4679837576537302652)
XLA Ops:
  0.6 0.0 copy-start.1
  0.6 0.6 copy-done.1
  1.3 0.1 select_reduce_fusion
  1.4 1.1 %copy.10 = bf16[4,16,8,512]{3,2,0,1:T(8,128)(2,1)S(1)} copy(bf16[4,16,8,512]{3,2,1,0:T(8,128)(2,1)} %bitcast.10) | data formatting | bytes 1048576 | tf_op jit(solution)/shard_map/reshape | solution.py:371
  2.5 0.6 gather_fusion
  3.1 0.1 broadcast_select_fusion.outgoing
  3.2 0.0 copy-start
  3.2 57.9 %shard_map.58 = (bf16[512,512]{1,0:T(8,128)(2,1)S(1)}, f32[1280,128]{1,0:T(8,128)S(1)}) custom-call(bf16[16,32,512]{2,1,0:T(8,128)(2,1)S(1)} %broadcast_select_fusion.outgoing), custom_call_target="tpu_custom_call" | custom-call | tf_op jit(solution)/shard_map/pallas_call | solution.py:202
  61.1 0.0 copy-done
  61.1 42.4 %shard_map.59 = (f32[512,512]{1,0:T(8,128)}, f32[512,128]{1,0:T(8,128)}, bf16[128,512]{1,0:T(8,128)(2,1)}) custom-call(f32[1280,128]{1,0:T(8,128)S(1)} %get-tuple-element.5.packed_ref, f32[512,128]{1,0:T(8,128)S(1)} %copy-done, bf16[512,512]{1,0:T(8,128)(2,1)S(1)} %get-tuple-element.6.columns_ref), custom_call_target="tpu_custom_call" | custom-call | tf_op jit(solution)/shard_map/pallas_call | solution.py:349
  (3 shorter events, 0.0 us)
Async XLA Ops:
  0.6 0.7 copy-start.1
  3.2 57.9 %copy-start = (f32[512,128]{1,0:T(8,128)S(1)}, f32[512,128]{1,0:T(8,128)}, u32[]{:S(2)}) copy-start(f32[512,128]{1,0:T(8,128)} %start_ref.1) | copy-start | bytes 786436
where the time goes:
time: 104 us
  Pallas kernels  100 us (96%)
  local copies, waits for them, and re-layouts  2.33 us (2%)
    pallas_call x1, Pallas kernels, exchange(): pl.pallas_call(functools.partial(exchange_kernel, sizes), out_shape=(jax....  57.9 us
    pallas_call x1, Pallas kernels, factor(): pl.pallas_call(factor_kernel, out_shape=(jax.ShapeDtypeStruct((rows, rows...  42.4 us

commit v1 on v0

--- a/solution.py
+++ b/solution.py
@@ -17,8 +17,8 @@
 
 
 def exchange_kernel(
-    sizes, outgoing, columns_ref, gram_ref,
-    part, pair_land, pair_sum, x_land, x_sum, y_land, z_land, y_gather, x_gather,
+    sizes, outgoing, columns_ref, pieces_ref,
+    part, pair_land, pair_sum, x_land, x_sum, y_land, z_land,
     a2a_send, a2a_recv, pair_send, pair_recv, x_send, x_recv, y_send, y_recv, z_send, z_recv,
     yg_send, yg_recv, xg_send, xg_recv, final_send, final_recv,
 ):
@@ -143,47 +143,74 @@
     for index in range(1, z_size):
         total = total + z_land[index]
 
-    y_gather[y] = total
-    copies = []
-    for step in ring_offsets(y_size):
-        peer = (y + step) % y_size
+    pieces_ref[core, x, y] = total
+    near = sorted(range(1, y_size), key=lambda step: min(step, y_size - step))
+    sent = []
+
+    def send(where, sems, index, target):
+        slot = pieces_ref.at[where]
         copy = pltpu.make_async_remote_copy(
-            src_ref=y_gather.at[y], dst_ref=y_gather.at[y],
-            send_sem=yg_send.at[step - 1], recv_sem=yg_recv.at[step - 1],
-            device_id={"gz": peer}, device_id_type=MESH,
+            src_ref=slot, dst_ref=slot, send_sem=sems[0].at[index], recv_sem=sems[1].at[index],
+            device_id=target, device_id_type=MESH,
         )
         copy.start()
-        copies.append(copy)
-    for copy in copies:
-        copy.wait()
-    my_x = pl.multiple_of(x * x_rows, x_rows)
-    for owner in range(y_size):
-        first = tile_start(owner)
-        last = tile_start(owner + 1) if owner + 1 < y_size else x_rows
-        x_gather[pl.ds(pl.multiple_of(my_x + first, 8), last - first), :] = y_gather[owner, : last - first, :]
-
-    copies = []
-    mine = pl.ds(my_x, x_rows)
-    for step in ring_offsets(x_size):
-        peer = (x + step) % x_size
-        copy = pltpu.make_async_remote_copy(
-            src_ref=x_gather.at[mine], dst_ref=x_gather.at[mine],
-            send_sem=xg_send.at[step - 1], recv_sem=xg_recv.at[step - 1],
-            device_id={"gy": peer}, device_id_type=MESH,
-        )
-        copy.start()
-        copies.append(copy)
-    for copy in copies:
-        copy.wait()
-
-    final = pltpu.make_async_remote_copy(
-        src_ref=x_gather, dst_ref=gram_ref.at[my_half],
-        send_sem=final_send, recv_sem=final_recv,
-        device_id={"af": fiber_at(0, 1)}, device_id_type=MESH,
-    )
-    final.start()
-    gram_ref[my_half, :] = x_gather[...]
-    final.wait()
+        sent.append(copy)
+
+    def wait_for(where, sems, index, target):
+        slot = pieces_ref.at[where]
+        pltpu.make_async_remote_copy(
+            src_ref=slot, dst_ref=slot, send_sem=sems[0].at[index], recv_sem=sems[1].at[index],
+            device_id=target, device_id_type=MESH,
+        ).wait_recv()
+
+    partner = {"af": fiber_at(0, 1)}
+    other = (core + 1) % 2
+    for step in reversed(near):
+        send((core, x, y), (yg_send, yg_recv), step - 1, {"gz": (y + step) % y_size})
+    for place in range(y_size):
+        owner = y
+        if place > 0:
+            step = near[place - 1]
+            owner = (y + y_size - step) % y_size
+            wait_for((core, x, owner), (yg_send, yg_recv), step - 1, {"gz": owner})
+        for step in ring_offsets(x_size):
+            send((core, x, owner), (xg_send, xg_recv), (step - 1) * y_size + place, {"gy": (x + step) % x_size})
+        send((core, x, owner), (final_send, final_recv), place, partner)
+    for place in range(y_size):
+        owner = (y + y_size - near[place - 1]) % y_size if place > 0 else y
+        for step in sorted(range(1, x_size), key=lambda step: min(step, x_size - step)):
+            origin = (x + x_size - step) % x_size
+            wait_for((core, origin, owner), (xg_send, xg_recv), (step - 1) * y_size + place, {"gy": origin})
+            send((core, origin, owner), (final_send, final_recv), step * y_size + place, partner)
+    for place in range(y_size):
+        owner = (y + y_size - near[place - 1]) % y_size if place > 0 else y
+        for step in range(x_size):
+            origin = (x + x_size - step) % x_size
+            wait_for((other, origin, owner), (final_send, final_recv), step * y_size + place, partner)
+    for copy in sent:
+        copy.wait_send()
+
+
+def arrange_kernel(owner_ref, slab_ref, out_ref):
+    fibers, _, block_cols = out_ref.shape
+    for target in range(fibers):
+        source = jnp.int32(0)
+        for block in range(1, fibers):
+            source = source + jnp.where(owner_ref[block] == target, block, 0)
+        start = pl.multiple_of(source * block_cols, block_cols)
+        out_ref[target] = slab_ref[:, pl.ds(start, block_cols)]
+
+
+def arrange(owners, slab):
+    fibers = owners.shape[0]
+    rows, width = slab.shape
+    return pl.pallas_call(
+        arrange_kernel,
+        out_shape=jax.ShapeDtypeStruct((fibers, rows, width // fibers), slab.dtype),
+        in_specs=[pl.BlockSpec(memory_space=pltpu.SMEM), pl.BlockSpec(memory_space=pltpu.VMEM)],
+        out_specs=pl.BlockSpec(memory_space=pltpu.VMEM),
+        compiler_params=pltpu.CompilerParams(vmem_limit_bytes=16 << 20),
+    )(owners, slab)
 
 
 def exchange(arranged):
@@ -203,7 +230,7 @@
         functools.partial(exchange_kernel, sizes),
         out_shape=(
             jax.ShapeDtypeStruct((all_rows, block_cols), bf16),
-            jax.ShapeDtypeStruct((2 * half, TILE), f32),
+            jax.ShapeDtypeStruct((2, x_size, y_size, y_rows, TILE), f32),
         ),
         in_specs=[pl.BlockSpec(memory_space=pltpu.VMEM)],
         out_specs=[pl.BlockSpec(memory_space=pltpu.VMEM)] * 2,
@@ -215,15 +242,41 @@
             pltpu.VMEM((x_rows, TILE), f32),
             pltpu.VMEM((y_size - 1, y_rows, TILE), f32),
             pltpu.VMEM((z_size, y_rows, TILE), f32),
-            pltpu.VMEM((y_size, y_rows, TILE), f32),
-            pltpu.VMEM((half, TILE), f32),
             dma((fibers - 1,)), dma((fibers - 1,)), dma, dma,
             dma((x_size - 1,)), dma((x_size - 1,)), dma((y_size - 1,)), dma((y_size - 1,)),
             dma((z_size - 1,)), dma((z_size - 1,)),
-            dma((y_size - 1,)), dma((y_size - 1,)), dma((x_size - 1,)), dma((x_size - 1,)), dma, dma,
+            dma((y_size - 1,)), dma((y_size - 1,)),
+            dma(((x_size - 1) * y_size,)), dma(((x_size - 1) * y_size,)),
+            dma((x_size * y_size,)), dma((x_size * y_size,)),
         ],
         compiler_params=pltpu.CompilerParams(collective_id=0, has_side_effects=True, vmem_limit_bytes=32 << 20),
     )(arranged)
+
+
+NN, NT, TN = ((1,), (0,)), ((1,), (1,)), ((0,), (0,))
+
+
+def parts_of(a):
+    f32, bf16 = jnp.float32, jnp.bfloat16
+    high = a.astype(bf16).astype(f32)
+    rest = a - high
+    middle = rest.astype(bf16).astype(f32)
+    return high, middle, rest - middle
+
+
+def stacked(a, order, axis):
+    parts = parts_of(a)
+    return jnp.concatenate([parts[k] for k in order], axis=axis).astype(jnp.bfloat16)
+
+
+LEFT, RIGHT = (0, 0, 1, 1, 0, 2), (0, 1, 0, 1, 2, 0)
+
+
+def dot_exact(a, b, dims):
+    (da,), (db,) = dims
+    return lax.dot_general(
+        stacked(a, LEFT, da), stacked(b, RIGHT, db), (dims, ((), ())), preferred_element_type=jnp.float32
+    )
 
 
 def eliminate_strip(work, final, scales, first):
@@ -232,8 +285,9 @@
     lane = lax.broadcasted_iota(jnp.int32, shape, 1)
     sub = lax.broadcasted_iota(jnp.int32, shape, 0)
     strip = work[pl.ds(first, STRIP), :]
-    rolled = pltpu.roll(strip, TILE - first, 1)
-    heads = [jnp.broadcast_to(rolled[:, t : t + 1], shape) for t in range(STRIP)]
+    heads = [
+        jnp.take_along_axis(strip, jnp.full(shape, first + t, jnp.int32), axis=1) for t in range(STRIP)
+    ]
     full = strip
     down = strip
     scale = jnp.zeros(shape, f32)
@@ -253,27 +307,24 @@
             heads[u] = jnp.where(sub == t, line * inverse, heads[u] - factor * line)
     final[pl.ds(first, STRIP), :] = down * scale
     scales[pl.ds(first, STRIP), :] = scale
-    return full
-
-
-def strip_update(work, full, first):
+    later = jnp.where(lane >= first + STRIP, strip, 0.0)
+    return full, later
+
+
+def strip_update(work, full, later, first):
     lane = lax.broadcasted_iota(jnp.int32, (TILE, TILE), 1)
-    sub = lax.broadcasted_iota(jnp.int32, (TILE, TILE), 0)
-    rows = work[...]
     own = (lane >= first) & (lane < first + STRIP)
-    below = sub >= first + STRIP
-    head = pltpu.roll(rows, TILE - first, 1)[:, :STRIP]
-    update = jnp.dot(head, full, precision=exact_mode, preferred_element_type=jnp.float32)
-    work[...] = jnp.where(below, jnp.where(own, 0.0, rows) - update, rows)
+    update = dot_exact(later, full, TN)
+    work[...] = jnp.where(own, 0.0, work[...]) - update
 
 
 def factor_both(works, finals, scales):
     @pl.loop(0, TILE // STRIP)
     def _(index):
         first = pl.multiple_of(index * STRIP, STRIP)
-        fulls = [eliminate_strip(w, f, s, first) for w, f, s in zip(works, finals, scales)]
-        for work, full in zip(works, fulls):
-            strip_update(work, full, first)
+        pieces = [eliminate_strip(w, f, s, first) for w, f, s in zip(works, finals, scales)]
+        for work, (full, later) in zip(works, pieces):
+            strip_update(work, full, later, first)
 
 
 def inverse_of(final, scales):
@@ -288,18 +339,19 @@
     return jnp.where(lane >= sub, final[...], 0.0)
 
 
-def dot_exact(a, b, dims):
-    return lax.dot_general(a, b, (dims, ((), ())), precision=exact_mode, preferred_element_type=jnp.float32)
-
-
-NN, NT, TN = ((1,), (0,)), ((1,), (1,)), ((0,), (0,))
-
-
 def factor_kernel(
-    packed_ref, start_ref, columns_ref, triangle_ref, basis_ref, core_ref,
-    gram, trail, product, work_a, work_b, final_a, final_b, scale_a, scale_b,
+    pieces_ref, start_ref, columns_ref, triangle_ref, basis_ref, core_ref,
+    packed_ref, gram, trail, product, work_a, work_b, final_a, final_b, scale_a, scale_b,
 ):
     count = 4
+    cores, x_size, y_size, _, _ = pieces_ref.shape
+    tiles = packed_ref.shape[0] // 8 // cores // x_size
+    for c in range(cores):
+        for x in range(x_size):
+            for y in range(y_size):
+                first, last = tiles * y // y_size, tiles * (y + 1) // y_size
+                spread = pl.ds(((c * x_size + x) * tiles + first) * 8, (last - first) * 8)
+                packed_ref[spread, :] = pieces_ref[c, x, y, : (last - first) * 8, :]
     spot = lambda i, j: pl.ds((i * (i + 1) // 2 + j) * TILE, TILE)
     at = lambda i: pl.ds(i * TILE, TILE)
     for i in range(count):
@@ -342,7 +394,7 @@
                 trail[tail, at(j)] = trail[tail, at(j)] - dot_exact(lower[skip:], lower[skip : skip + TILE], NT)
 
 
-def factor(packed, start, columns):
+def factor(pieces, start, columns):
     f32 = jnp.float32
     rows, rank = start.shape
     square = pltpu.VMEM((TILE, TILE), f32)
@@ -356,20 +408,15 @@
         in_specs=[pl.BlockSpec(memory_space=pltpu.VMEM)] * 3,
         out_specs=[pl.BlockSpec(memory_space=pltpu.VMEM)] * 3,
         scratch_shapes=[
-            pltpu.VMEM((rows, rows), f32), pltpu.VMEM((rows, rows), f32), pltpu.VMEM((rows, rank), f32),
+            pltpu.VMEM((10 * TILE, TILE), f32), pltpu.VMEM((rows, rows), f32), pltpu.VMEM((rows, rows), f32), pltpu.VMEM((rows, rank), f32),
             square, square, square, square, square, square,
         ],
         compiler_params=pltpu.CompilerParams(vmem_limit_bytes=32 << 20),
-    )(packed, start, columns)
+    )(pieces, start, columns)
 
 
 def on_device(slab, block_owner, basis_init):
-    fibers = lax.axis_size("af")
-    labels = jnp.arange(fibers, dtype=jnp.int32)
-    onehot = (block_owner.reshape(fibers)[:, None] == labels[None, :]).astype(jnp.int32)
-    source = jnp.sum(onehot * labels[:, None], axis=0)
-    pieces = slab.reshape(slab.shape[0], fibers, -1)
-    columns, packed = exchange(jnp.take(pieces, source, axis=1).transpose(1, 0, 2))
+    columns, packed = exchange(arrange(block_owner.reshape(-1), slab))
     return factor(packed, basis_init, columns)
 
 

time: 104 us -> 92.1 us (0.89)
  Pallas kernels: 100 us -> 89.6 us
    pallas_call x1, Pallas kernels: 42.4 us -> 29.7 us  [factor(): pl.pallas_call(factor_kernel, out_shape=(jax.ShapeDtypeStruct((rows, rows...]
    pallas_call x1, Pallas kernels: 57.9 us -> 59 us  [exchange(): pl.pallas_call(functools.partial(exchange_kernel, sizes), out_shape=(jax....]
    reshape x1 -> x0, local copies, waits for them, and re-layouts: 1.09 us -> none  [on_device(): pieces = slab.reshape(slab.shape[0], fibers, -1)]
    unnamed x4 -> x6, local copies, waits for them, and re-layouts: 0.65 us -> 1.7 us
where the time goes in v1:
time: 92.1 us; the launch traced here: 92 us
  Pallas kernels  89.6 us (97%)
  local copies, waits for them, and re-layouts  1.7 us (2%)
    pallas_call x1, Pallas kernels, exchange(): pl.pallas_call(functools.partial(exchange_kernel, sizes), out_shape=(jax....  59 us
    pallas_call x1, Pallas kernels, factor(): pl.pallas_call(factor_kernel, out_shape=(jax.ShapeDtypeStruct((rows, rows...  29.7 us

profile of v1, /device:TPU:1, one launch (start us, length us, event | category | flops | bytes accessed | tf_op | source)
XLA Modules:
  0.0 92.0 jit_solution(9375224527624985864)
XLA Ops:
  0.6 0.0 copy-start.2
  0.6 0.6 copy-done.2
  1.3 0.0 copy-start
  1.3 1.0 %copy-done = bf16[32,8192]{1,0:T(8,128)(2,1)S(1)} copy-done((bf16[32,8192]{1,0:T(8,128)(2,1)S(1)}, bf16[32,8192]{1,0:T(8,128)(2,1)}, u32[]{:S(2)}) %copy-start) | copy-done | bytes 524312
  2.3 0.8 shard_map.58.outgoing
  3.2 0.0 copy-start.1
  3.2 59.0 %shard_map.59 = (bf16[512,512]{1,0:T(8,128)(2,1)S(1)}, f32[2,4,8,24,128]{4,3,2,1,0:T(8,128)S(1)}) custom-call(bf16[16,32,512]{2,1,0:T(8,128)(2,1)S(1)} %shard_map.58.outgoing), custom_call_target="tpu_custom_call" | custom-call | tf_op jit(solution)/shard_map/pallas_call | solution.py:229
  62.2 0.0 copy-done.1
  62.2 29.7 %shard_map.60 = (f32[512,512]{1,0:T(8,128)}, f32[512,128]{1,0:T(8,128)}, bf16[128,512]{1,0:T(8,128)(2,1)}) custom-call(f32[2,4,8,24,128]{4,3,2,1,0:T(8,128)S(1)} %get-tuple-element.5.pieces_ref, f32[512,128]{1,0:T(8,128)S(1)} %copy-done.1, bf16[512,512]{1,0:T(8,128)(2,1)S(1)} %get-tuple-element.6.columns_ref), custom_call_target="tpu_custom_call" | custom-call | tf_op jit(solution)/shard_map/pallas_call | solution.py:401
Async XLA Ops:
  0.6 0.7 copy-start.2
  1.3 1.0 %copy-start = (bf16[32,8192]{1,0:T(8,128)(2,1)S(1)}, bf16[32,8192]{1,0:T(8,128)(2,1)}, u32[]{:S(2)}) copy-start(bf16[32,8192]{1,0:T(8,128)(2,1)} %slab_ref.1) | copy-start | bytes 1572868
  3.2 59.1 %copy-start.1 = (f32[512,128]{1,0:T(8,128)S(1)}, f32[512,128]{1,0:T(8,128)}, u32[]{:S(2)}) copy-start(f32[512,128]{1,0:T(8,128)} %start_ref.1) | copy-start | bytes 786436

commit v2 on v1

--- a/solution.py
+++ b/solution.py
@@ -36,7 +36,7 @@
     def fiber_at(z_step, core_step):
         return ((z + z_step) % z_size) * 2 + (core + core_step) % 2
 
-    fiber_steps = [(s, c) for s in ring_offsets(z_size) for c in (0, 1)] + [(0, 1)]
+    fiber_steps = [(0, 1)] + [(s, c) for s in reversed(ring_offsets(z_size)) for c in (0, 1)]
     barrier = pltpu.get_barrier_semaphore()
     for z_step, core_step in fiber_steps:
         pl.semaphore_signal(barrier, inc=1, device_id={"af": fiber_at(z_step, core_step)}, device_id_type=MESH)
@@ -143,73 +143,83 @@
     for index in range(1, z_size):
         total = total + z_land[index]
 
-    pieces_ref[core, x, y] = total
+    pieces_ref[core, x, 0] = total
     near = sorted(range(1, y_size), key=lambda step: min(step, y_size - step))
     sent = []
 
-    def send(where, sems, index, target):
-        slot = pieces_ref.at[where]
-        copy = pltpu.make_async_remote_copy(
-            src_ref=slot, dst_ref=slot, send_sem=sems[0].at[index], recv_sem=sems[1].at[index],
+    def copy_of(src, dst, sems, index, target):
+        return pltpu.make_async_remote_copy(
+            src_ref=pieces_ref.at[src], dst_ref=pieces_ref.at[dst],
+            send_sem=sems[0].at[index], recv_sem=sems[1].at[index],
             device_id=target, device_id_type=MESH,
         )
+
+    def send(*args):
+        copy = copy_of(*args)
         copy.start()
         sent.append(copy)
 
-    def wait_for(where, sems, index, target):
-        slot = pieces_ref.at[where]
-        pltpu.make_async_remote_copy(
-            src_ref=slot, dst_ref=slot, send_sem=sems[0].at[index], recv_sem=sems[1].at[index],
-            device_id=target, device_id_type=MESH,
-        ).wait_recv()
-
+    y_sems, x_sems, pair_sems = (yg_send, yg_recv), (xg_send, xg_recv), (final_send, final_recv)
     partner = {"af": fiber_at(0, 1)}
     other = (core + 1) % 2
-    for step in reversed(near):
-        send((core, x, y), (yg_send, yg_recv), step - 1, {"gz": (y + step) % y_size})
-    for place in range(y_size):
-        owner = y
-        if place > 0:
-            step = near[place - 1]
-            owner = (y + y_size - step) % y_size
-            wait_for((core, x, owner), (yg_send, yg_recv), step - 1, {"gz": owner})
-        for step in ring_offsets(x_size):
-            send((core, x, owner), (xg_send, xg_recv), (step - 1) * y_size + place, {"gy": (x + step) % x_size})
-        send((core, x, owner), (final_send, final_recv), place, partner)
-    for place in range(y_size):
-        owner = (y + y_size - near[place - 1]) % y_size if place > 0 else y
-        for step in sorted(range(1, x_size), key=lambda step: min(step, x_size - step)):
+    for place in range(y_size - 1, 0, -1):
+        target = {"gz": (y + near[place - 1]) % y_size}
+        send((core, x, 0), (core, x, place), y_sems, place - 1, target)
+    groups = [pl.ds(0, y_size // 2), pl.ds(y_size // 2, y_size // 2)]
+    x_steps = sorted(range(1, x_size), key=lambda step: min(step, x_size - step))
+    for number, group in enumerate(groups):
+        for place in range(max(group.start, 1), group.start + group.size):
+            target = {"gz": (y + near[place - 1]) % y_size}
+            copy_of((core, x, 0), (core, x, place), y_sems, place - 1, target).wait_recv()
+        mine = (core, x, group)
+        for step in reversed(x_steps):
+            send(mine, mine, x_sems, (step - 1) * 2 + number, {"gy": (x + step) % x_size})
+        send(mine, mine, pair_sems, number, partner)
+    for number, group in enumerate(groups):
+        for step in x_steps:
             origin = (x + x_size - step) % x_size
-            wait_for((core, origin, owner), (xg_send, xg_recv), (step - 1) * y_size + place, {"gy": origin})
-            send((core, origin, owner), (final_send, final_recv), step * y_size + place, partner)
-    for place in range(y_size):
-        owner = (y + y_size - near[place - 1]) % y_size if place > 0 else y
+            theirs = (core, origin, group)
+            copy_of(theirs, theirs, x_sems, (step - 1) * 2 + number, {"gy": origin}).wait_recv()
+            send(theirs, theirs, pair_sems, step * 2 + number, partner)
+    for number, group in enumerate(groups):
         for step in range(x_size):
-            origin = (x + x_size - step) % x_size
-            wait_for((other, origin, owner), (final_send, final_recv), step * y_size + place, partner)
+            theirs = (other, (x + x_size - step) % x_size, group)
+            copy_of(theirs, theirs, pair_sems, step * 2 + number, partner).wait_recv()
     for copy in sent:
         copy.wait_send()
 
 
-def arrange_kernel(owner_ref, slab_ref, out_ref):
+def arrange_kernel(owner_ref, slab_ref, out_ref, owners, slab, sems):
     fibers, _, block_cols = out_ref.shape
+    loads = [
+        pltpu.make_async_copy(owner_ref, owners, sems.at[0]),
+        pltpu.make_async_copy(slab_ref, slab, sems.at[1]),
+    ]
+    for load in loads:
+        load.start()
+    loads[0].wait()
+    starts = []
     for target in range(fibers):
         source = jnp.int32(0)
         for block in range(1, fibers):
-            source = source + jnp.where(owner_ref[block] == target, block, 0)
-        start = pl.multiple_of(source * block_cols, block_cols)
-        out_ref[target] = slab_ref[:, pl.ds(start, block_cols)]
+            source = source + jnp.where(owners[0, 0, block] == target, block, 0)
+        starts.append(pl.multiple_of(source * block_cols, block_cols))
+    loads[1].wait()
+    for target in range(fibers):
+        out_ref[target] = slab[:, pl.ds(starts[target], block_cols)]
 
 
 def arrange(owners, slab):
-    fibers = owners.shape[0]
+    fibers = owners.shape[-1]
     rows, width = slab.shape
     return pl.pallas_call(
         arrange_kernel,
         out_shape=jax.ShapeDtypeStruct((fibers, rows, width // fibers), slab.dtype),
-        in_specs=[pl.BlockSpec(memory_space=pltpu.SMEM), pl.BlockSpec(memory_space=pltpu.VMEM)],
+        in_specs=[pl.BlockSpec(memory_space=pl.ANY)] * 2,
         out_specs=pl.BlockSpec(memory_space=pltpu.VMEM),
-        compiler_params=pltpu.CompilerParams(vmem_limit_bytes=16 << 20),
+        scratch_shapes=[
+            pltpu.SMEM(owners.shape, jnp.int32), pltpu.VMEM(slab.shape, slab.dtype), pltpu.SemaphoreType.DMA((2,)),
+        ],
     )(owners, slab)
 
 
@@ -246,8 +256,8 @@
             dma((x_size - 1,)), dma((x_size - 1,)), dma((y_size - 1,)), dma((y_size - 1,)),
             dma((z_size - 1,)), dma((z_size - 1,)),
             dma((y_size - 1,)), dma((y_size - 1,)),
-            dma(((x_size - 1) * y_size,)), dma(((x_size - 1) * y_size,)),
-            dma((x_size * y_size,)), dma((x_size * y_size,)),
+            dma(((x_size - 1) * 2,)), dma(((x_size - 1) * 2,)),
+            dma((x_size * 2,)), dma((x_size * 2,)),
         ],
         compiler_params=pltpu.CompilerParams(collective_id=0, has_side_effects=True, vmem_limit_bytes=32 << 20),
     )(arranged)
@@ -270,12 +280,13 @@
 
 
 LEFT, RIGHT = (0, 0, 1, 1, 0, 2), (0, 1, 0, 1, 2, 0)
-
-
-def dot_exact(a, b, dims):
+MID = 4
+
+
+def dot_exact(a, b, dims, terms=6):
     (da,), (db,) = dims
     return lax.dot_general(
-        stacked(a, LEFT, da), stacked(b, RIGHT, db), (dims, ((), ())), preferred_element_type=jnp.float32
+        stacked(a, LEFT[:terms], da), stacked(b, RIGHT[:terms], db), (dims, ((), ())), preferred_element_type=jnp.float32
     )
 
 
@@ -346,12 +357,16 @@
     count = 4
     cores, x_size, y_size, _, _ = pieces_ref.shape
     tiles = packed_ref.shape[0] // 8 // cores // x_size
-    for c in range(cores):
-        for x in range(x_size):
-            for y in range(y_size):
+    here = lax.axis_index("gz")
+    for y in range(y_size):
+        step = (here + y_size - y) % y_size
+        near = jnp.minimum(step, y_size - step)
+        place = 2 * near - jnp.where((step > 0) & (step <= y_size // 2), 1, 0)
+        for c in range(cores):
+            for x in range(x_size):
                 first, last = tiles * y // y_size, tiles * (y + 1) // y_size
                 spread = pl.ds(((c * x_size + x) * tiles + first) * 8, (last - first) * 8)
-                packed_ref[spread, :] = pieces_ref[c, x, y, : (last - first) * 8, :]
+                packed_ref[spread, :] = pieces_ref[c, x, place, : (last - first) * 8, :]
     spot = lambda i, j: pl.ds((i * (i + 1) // 2 + j) * TILE, TILE)
     at = lambda i: pl.ds(i * TILE, TILE)
     for i in range(count):
@@ -363,21 +378,21 @@
                 gram[at(j), at(i)] = block.T
                 triangle_ref[at(j), at(i)] = jnp.zeros((TILE, TILE), jnp.float32)
     start = start_ref[...]
-    image = dot_exact(gram[...], start, NN)
+    image = dot_exact(gram[...], start, NN, MID)
     product[...] = image
-    work_b[...] = dot_exact(start, image, TN)
+    work_b[...] = dot_exact(start, image, TN, MID)
     for k in range(count):
         work_a[...] = trail[at(k), at(k)]
         factor_both((work_a, work_b), (final_a, final_b), (scale_a, scale_b))
         turn = inverse_of(final_b, scale_b)
-        image = dot_exact(product[...], turn, NT)
+        image = dot_exact(product[...], turn, NT, 6 if k == count - 1 else MID)
         if k == 0 or k == 2:
             product[...] = image
-            work_b[...] = dot_exact(image, image, TN)
+            work_b[...] = dot_exact(image, image, TN, 6 if k == 2 else MID)
         elif k == 1:
-            moved = dot_exact(gram[...], image, NN)
+            moved = dot_exact(gram[...], image, NN, MID)
             product[...] = moved
-            work_b[...] = dot_exact(image, moved, TN)
+            work_b[...] = dot_exact(image, moved, TN, MID)
         else:
             basis_ref[...] = image
             core_ref[...] = lax.dot_general(
@@ -416,7 +431,7 @@
 
 
 def on_device(slab, block_owner, basis_init):
-    columns, packed = exchange(arrange(block_owner.reshape(-1), slab))
+    columns, packed = exchange(arrange(block_owner, slab))
     return factor(packed, basis_init, columns)
 
 

time: 92.1 us -> 89.9 us (0.976)
  Pallas kernels: 89.6 us -> 88.1 us
    pallas_call x1, Pallas kernels: 29.7 us -> 28 us  [factor(): pl.pallas_call(factor_kernel, out_shape=(jax.ShapeDtypeStruct((rows, rows...]
    pallas_call x1, Pallas kernels: 0.83 us -> 1.89 us  [arrange(): pl.pallas_call(arrange_kernel, out_shape=jax.ShapeDtypeStruct((fibers, ro...]
where the time goes in v2:
time: 89.9 us; the launch traced here: 89.8 us
  Pallas kernels  88.1 us (98%)
  local copies, waits for them, and re-layouts  1.04 us (1%)
    pallas_call x1, Pallas kernels, exchange(): pl.pallas_call(functools.partial(exchange_kernel, sizes), out_shape=(jax....  58.2 us
    pallas_call x1, Pallas kernels, factor(): pl.pallas_call(factor_kernel, out_shape=(jax.ShapeDtypeStruct((rows, rows...  28 us
    pallas_call x1, Pallas kernels, arrange(): pl.pallas_call(arrange_kernel, out_shape=jax.ShapeDtypeStruct((fibers, ro...  1.89 us

profile of v2, /device:TPU:1, one launch (start us, length us, event | category | flops | bytes accessed | tf_op | source)
XLA Modules:
  0.0 89.8 jit_solution(6591060299326916878)
XLA Ops:
  0.6 1.9 %shard_map.58.outgoing = bf16[16,32,512]{2,1,0:T(8,128)(2,1)} custom-call(s32[1,1,16]{2,1,0:T(1,128)} %owner_ref.1, bf16[32,8192]{1,0:T(8,128)(2,1)} %slab_ref.1), custom_call_target="tpu_custom_call" | custom-call | tf_op jit(solution)/shard_map/pallas_call | solution.py:215
  2.5 0.0 copy-start
  2.5 1.0 %copy-done = bf16[16,32,512]{2,1,0:T(8,128)(2,1)S(1)} copy-done((bf16[16,32,512]{2,1,0:T(8,128)(2,1)S(1)}, bf16[16,32,512]{2,1,0:T(8,128)(2,1)}, u32[]{:S(2)}) %copy-start) | copy-done | bytes 524312
  3.6 0.0 copy-start.1
  3.6 58.2 %shard_map.59 = (bf16[512,512]{1,0:T(8,128)(2,1)S(1)}, f32[2,4,8,24,128]{4,3,2,1,0:T(8,128)S(1)}) custom-call(bf16[16,32,512]{2,1,0:T(8,128)(2,1)S(1)} %copy-done), custom_call_target="tpu_custom_call" | custom-call | tf_op jit(solution)/shard_map/pallas_call | solution.py:239
  61.7 0.0 copy-done.1
  61.8 28.0 %shard_map.60 = (f32[512,512]{1,0:T(8,128)}, f32[512,128]{1,0:T(8,128)}, bf16[128,512]{1,0:T(8,128)(2,1)}) custom-call(f32[2,4,8,24,128]{4,3,2,1,0:T(8,128)S(1)} %get-tuple-element.5.pieces_ref, f32[512,128]{1,0:T(8,128)S(1)} %copy-done.1, bf16[512,512]{1,0:T(8,128)(2,1)S(1)} %get-tuple-element.6.columns_ref), custom_call_target="tpu_custom_call" | custom-call | tf_op jit(solution)/shard_map/pallas_call | solution.py:416
Async XLA Ops:
  2.5 1.0 %copy-start = (bf16[16,32,512]{2,1,0:T(8,128)(2,1)S(1)}, bf16[16,32,512]{2,1,0:T(8,128)(2,1)}, u32[]{:S(2)}) copy-start(bf16[16,32,512]{2,1,0:T(8,128)(2,1)} %shard_map.58.outgoing) | copy-start | bytes 1572868
  3.6 58.2 %copy-start.1 = (f32[512,128]{1,0:T(8,128)S(1)}, f32[512,128]{1,0:T(8,128)}, u32[]{:S(2)}) copy-start(f32[512,128]{1,0:T(8,128)} %start_ref.1) | copy-start | bytes 786436

commit v3 on v2

--- a/solution.py
+++ b/solution.py
@@ -290,12 +290,11 @@
     )
 
 
-def eliminate_strip(work, final, scales, first):
+def eliminate_strip(strip, final, scales, first):
     f32 = jnp.float32
     shape = (STRIP, TILE)
     lane = lax.broadcasted_iota(jnp.int32, shape, 1)
     sub = lax.broadcasted_iota(jnp.int32, shape, 0)
-    strip = work[pl.ds(first, STRIP), :]
     heads = [
         jnp.take_along_axis(strip, jnp.full(shape, first + t, jnp.int32), axis=1) for t in range(STRIP)
     ]
@@ -318,24 +317,54 @@
             heads[u] = jnp.where(sub == t, line * inverse, heads[u] - factor * line)
     final[pl.ds(first, STRIP), :] = down * scale
     scales[pl.ds(first, STRIP), :] = scale
+    return full
+
+
+def stacked_wide(a, order):
+    parts = parts_of(a)
+    return jnp.concatenate([parts[k] for k in order], axis=0)
+
+
+def advance(strip, full, work, left, right, first):
+    shape = (STRIP, TILE)
+    lane = lax.broadcasted_iota(jnp.int32, shape, 1)
     later = jnp.where(lane >= first + STRIP, strip, 0.0)
-    return full, later
-
-
-def strip_update(work, full, later, first):
+    left[...] = stacked_wide(later, LEFT).astype(jnp.bfloat16).T
+    right[...] = stacked_wide(full, RIGHT).astype(jnp.bfloat16)
+    onward = pl.ds(pl.multiple_of(jnp.minimum(first + STRIP, TILE - STRIP), STRIP), STRIP)
+    own = (lane >= first) & (lane < first + STRIP)
+    following = jnp.where(own, 0.0, work[onward, :])
+    sub = lax.broadcasted_iota(jnp.int32, shape, 0)
+    change = jnp.zeros(shape, jnp.float32)
+    for s in range(STRIP):
+        spot = jnp.full(shape, jnp.minimum(first + STRIP + s, TILE - 1), jnp.int32)
+        line = jnp.sum(jnp.take_along_axis(strip, spot, axis=1) * full, axis=0, keepdims=True)
+        change = jnp.where(sub == s, jnp.broadcast_to(line, shape), change)
+    return following - change
+
+
+def apply_update(work, left, right, first):
     lane = lax.broadcasted_iota(jnp.int32, (TILE, TILE), 1)
-    own = (lane >= first) & (lane < first + STRIP)
-    update = dot_exact(later, full, TN)
-    work[...] = jnp.where(own, 0.0, work[...]) - update
-
-
-def factor_both(works, finals, scales):
-    @pl.loop(0, TILE // STRIP)
-    def _(index):
+    before = (lane >= first - STRIP) & (lane < first)
+    update = jnp.dot(left[...], right[...], preferred_element_type=jnp.float32)
+    work[...] = jnp.where(before, 0.0, work[...]) - update
+
+
+def factor_both(works, finals, scales, lefts, rights):
+    for left, right in zip(lefts, rights):
+        left[...] = jnp.zeros_like(left)
+        right[...] = jnp.zeros_like(right)
+
+    def step(index, strips):
         first = pl.multiple_of(index * STRIP, STRIP)
-        pieces = [eliminate_strip(w, f, s, first) for w, f, s in zip(works, finals, scales)]
-        for work, (full, later) in zip(works, pieces):
-            strip_update(work, full, later, first)
+        for work, left, right in zip(works, lefts, rights):
+            apply_update(work, left, right, first)
+        fulls = [eliminate_strip(v, f, s, first) for v, f, s in zip(strips, finals, scales)]
+        return tuple(
+            advance(*group, first) for group in zip(strips, fulls, works, lefts, rights)
+        )
+
+    lax.fori_loop(0, TILE // STRIP, step, tuple(work[:STRIP, :] for work in works))
 
 
 def inverse_of(final, scales):
@@ -353,6 +382,7 @@
 def factor_kernel(
     pieces_ref, start_ref, columns_ref, triangle_ref, basis_ref, core_ref,
     packed_ref, gram, trail, product, work_a, work_b, final_a, final_b, scale_a, scale_b,
+    left_a, left_b, right_a, right_b,
 ):
     count = 4
     cores, x_size, y_size, _, _ = pieces_ref.shape
@@ -383,7 +413,10 @@
     work_b[...] = dot_exact(start, image, TN, MID)
     for k in range(count):
         work_a[...] = trail[at(k), at(k)]
-        factor_both((work_a, work_b), (final_a, final_b), (scale_a, scale_b))
+        factor_both(
+            (work_a, work_b), (final_a, final_b), (scale_a, scale_b),
+            (left_a, left_b), (right_a, right_b),
+        )
         turn = inverse_of(final_b, scale_b)
         image = dot_exact(product[...], turn, NT, 6 if k == count - 1 else MID)
         if k == 0 or k == 2:
@@ -413,6 +446,7 @@
     f32 = jnp.float32
     rows, rank = start.shape
     square = pltpu.VMEM((TILE, TILE), f32)
+    wide, tall = pltpu.VMEM((TILE, 6 * STRIP), jnp.bfloat16), pltpu.VMEM((6 * STRIP, TILE), jnp.bfloat16)
     return pl.pallas_call(
         factor_kernel,
         out_shape=(
@@ -425,6 +459,7 @@
         scratch_shapes=[
             pltpu.VMEM((10 * TILE, TILE), f32), pltpu.VMEM((rows, rows), f32), pltpu.VMEM((rows, rows), f32), pltpu.VMEM((rows, rank), f32),
             square, square, square, square, square, square,
+            wide, wide, tall, tall,
         ],
         compiler_params=pltpu.CompilerParams(vmem_limit_bytes=32 << 20),
     )(pieces, start, columns)

time: 89.9 us -> 84.1 us (0.935)
  Pallas kernels: 88.1 us -> 82.2 us
    pallas_call x1, Pallas kernels: 28 us -> 22.1 us  [factor(): pl.pallas_call(factor_kernel, out_shape=(jax.ShapeDtypeStruct((rows, rows...]
where the time goes in v3:
time: 84.1 us; the launch traced here: 83.9 us
  Pallas kernels  82.2 us (98%)
  local copies, waits for them, and re-layouts  1.04 us (1%)
    pallas_call x1, Pallas kernels, exchange(): pl.pallas_call(functools.partial(exchange_kernel, sizes), out_shape=(jax....  58.2 us
    pallas_call x1, Pallas kernels, factor(): pl.pallas_call(factor_kernel, out_shape=(jax.ShapeDtypeStruct((rows, rows...  22.1 us
    pallas_call x1, Pallas kernels, arrange(): pl.pallas_call(arrange_kernel, out_shape=jax.ShapeDtypeStruct((fibers, ro...  1.89 us

profile of v3, /device:TPU:1, one launch (start us, length us, event | category | flops | bytes accessed | tf_op | source)
XLA Modules:
  0.0 83.9 jit_solution(6120431620016117696)
XLA Ops:
  0.6 1.9 %shard_map.58.outgoing = bf16[16,32,512]{2,1,0:T(8,128)(2,1)} custom-call(s32[1,1,16]{2,1,0:T(1,128)} %owner_ref.1, bf16[32,8192]{1,0:T(8,128)(2,1)} %slab_ref.1), custom_call_target="tpu_custom_call" | custom-call | tf_op jit(solution)/shard_map/pallas_call | solution.py:215
  2.5 0.0 copy-start
  2.5 1.0 %copy-done = bf16[16,32,512]{2,1,0:T(8,128)(2,1)S(1)} copy-done((bf16[16,32,512]{2,1,0:T(8,128)(2,1)S(1)}, bf16[16,32,512]{2,1,0:T(8,128)(2,1)}, u32[]{:S(2)}) %copy-start) | copy-done | bytes 524312
  3.6 0.0 copy-start.1
  3.6 58.2 %shard_map.59 = (bf16[512,512]{1,0:T(8,128)(2,1)S(1)}, f32[2,4,8,24,128]{4,3,2,1,0:T(8,128)S(1)}) custom-call(bf16[16,32,512]{2,1,0:T(8,128)(2,1)S(1)} %copy-done), custom_call_target="tpu_custom_call" | custom-call | tf_op jit(solution)/shard_map/pallas_call | solution.py:239
  61.7 0.0 copy-done.1
  61.8 22.1 %shard_map.60 = (f32[512,512]{1,0:T(8,128)}, f32[512,128]{1,0:T(8,128)}, bf16[128,512]{1,0:T(8,128)(2,1)}) custom-call(f32[2,4,8,24,128]{4,3,2,1,0:T(8,128)S(1)} %get-tuple-element.5.pieces_ref, f32[512,128]{1,0:T(8,128)S(1)} %copy-done.1, bf16[512,512]{1,0:T(8,128)(2,1)S(1)} %get-tuple-element.6.columns_ref), custom_call_target="tpu_custom_call" | custom-call | tf_op jit(solution)/shard_map/pallas_call | solution.py:450
Async XLA Ops:
  2.5 1.0 %copy-start = (bf16[16,32,512]{2,1,0:T(8,128)(2,1)S(1)}, bf16[16,32,512]{2,1,0:T(8,128)(2,1)}, u32[]{:S(2)}) copy-start(bf16[16,32,512]{2,1,0:T(8,128)(2,1)} %shard_map.58.outgoing) | copy-start | bytes 1572868
  3.6 58.2 %copy-start.1 = (f32[512,128]{1,0:T(8,128)S(1)}, f32[512,128]{1,0:T(8,128)}, u32[]{:S(2)}) copy-start(f32[512,128]{1,0:T(8,128)} %start_ref.1) | copy-start | bytes 786436

commit v4 on v3

--- a/solution.py
+++ b/solution.py
@@ -280,7 +280,7 @@
 
 
 LEFT, RIGHT = (0, 0, 1, 1, 0, 2), (0, 1, 0, 1, 2, 0)
-MID = 4
+MID = 3
 
 
 def dot_exact(a, b, dims, terms=6):
@@ -434,12 +434,12 @@
         triangle_ref[at(k), at(k)] = upper_of(final_a).T
         if k + 1 < count:
             rest = pl.ds((k + 1) * TILE, (count - 1 - k) * TILE)
-            lower = dot_exact(trail[rest, at(k)], inverse_of(final_a, scale_a), NT)
+            lower = dot_exact(trail[rest, at(k)], inverse_of(final_a, scale_a), NT, 4)
             triangle_ref[rest, at(k)] = lower
             for j in range(k + 1, count):
                 tail = pl.ds(j * TILE, (count - j) * TILE)
                 skip = (j - k - 1) * TILE
-                trail[tail, at(j)] = trail[tail, at(j)] - dot_exact(lower[skip:], lower[skip : skip + TILE], NT)
+                trail[tail, at(j)] = trail[tail, at(j)] - dot_exact(lower[skip:], lower[skip : skip + TILE], NT, 4)
 
 
 def factor(pieces, start, columns):

time: 84.1 us -> 82.3 us (0.979)
  Pallas kernels: 82.2 us -> 80.4 us
    pallas_call x1, Pallas kernels: 22.1 us -> 20.4 us  [factor(): pl.pallas_call(factor_kernel, out_shape=(jax.ShapeDtypeStruct((rows, rows...]
where the time goes in v4:
time: 82.3 us; the launch traced here: 82.1 us
  Pallas kernels  80.4 us (98%)
  local copies, waits for them, and re-layouts  1.04 us (1%)
    pallas_call x1, Pallas kernels, exchange(): pl.pallas_call(functools.partial(exchange_kernel, sizes), out_shape=(jax....  58.2 us
    pallas_call x1, Pallas kernels, factor(): pl.pallas_call(factor_kernel, out_shape=(jax.ShapeDtypeStruct((rows, rows...  20.4 us
    pallas_call x1, Pallas kernels, arrange(): pl.pallas_call(arrange_kernel, out_shape=jax.ShapeDtypeStruct((fibers, ro...  1.89 us

profile of v4, /device:TPU:1, one launch (start us, length us, event | category | flops | bytes accessed | tf_op | source)
XLA Modules:
  0.0 82.1 jit_solution(7301612387031660313)
XLA Ops:
  0.6 1.9 %shard_map.58.outgoing = bf16[16,32,512]{2,1,0:T(8,128)(2,1)} custom-call(s32[1,1,16]{2,1,0:T(1,128)} %owner_ref.1, bf16[32,8192]{1,0:T(8,128)(2,1)} %slab_ref.1), custom_call_target="tpu_custom_call" | custom-call | tf_op jit(solution)/shard_map/pallas_call | solution.py:215
  2.5 0.0 copy-start
  2.5 1.0 %copy-done = bf16[16,32,512]{2,1,0:T(8,128)(2,1)S(1)} copy-done((bf16[16,32,512]{2,1,0:T(8,128)(2,1)S(1)}, bf16[16,32,512]{2,1,0:T(8,128)(2,1)}, u32[]{:S(2)}) %copy-start) | copy-done | bytes 524312
  3.6 0.0 copy-start.1
  3.6 58.2 %shard_map.59 = (bf16[512,512]{1,0:T(8,128)(2,1)S(1)}, f32[2,4,8,24,128]{4,3,2,1,0:T(8,128)S(1)}) custom-call(bf16[16,32,512]{2,1,0:T(8,128)(2,1)S(1)} %copy-done), custom_call_target="tpu_custom_call" | custom-call | tf_op jit(solution)/shard_map/pallas_call | solution.py:239
  61.7 0.0 copy-done.1
  61.8 20.4 %shard_map.60 = (f32[512,512]{1,0:T(8,128)}, f32[512,128]{1,0:T(8,128)}, bf16[128,512]{1,0:T(8,128)(2,1)}) custom-call(f32[2,4,8,24,128]{4,3,2,1,0:T(8,128)S(1)} %get-tuple-element.5.pieces_ref, f32[512,128]{1,0:T(8,128)S(1)} %copy-done.1, bf16[512,512]{1,0:T(8,128)(2,1)S(1)} %get-tuple-element.6.columns_ref), custom_call_target="tpu_custom_call" | custom-call | tf_op jit(solution)/shard_map/pallas_call | solution.py:450
Async XLA Ops:
  2.5 1.0 %copy-start = (bf16[16,32,512]{2,1,0:T(8,128)(2,1)S(1)}, bf16[16,32,512]{2,1,0:T(8,128)(2,1)}, u32[]{:S(2)}) copy-start(bf16[16,32,512]{2,1,0:T(8,128)(2,1)} %shard_map.58.outgoing) | copy-start | bytes 1572868
  3.6 58.2 %copy-start.1 = (f32[512,128]{1,0:T(8,128)S(1)}, f32[512,128]{1,0:T(8,128)}, u32[]{:S(2)}) copy-start(f32[512,128]{1,0:T(8,128)} %start_ref.1) | copy-start | bytes 786436

commit v5 on v4

--- a/solution.py
+++ b/solution.py
@@ -364,7 +364,7 @@
             advance(*group, first) for group in zip(strips, fulls, works, lefts, rights)
         )
 
-    lax.fori_loop(0, TILE // STRIP, step, tuple(work[:STRIP, :] for work in works))
+    lax.fori_loop(0, TILE // STRIP, step, tuple(work[:STRIP, :] for work in works), unroll=4)
 
 
 def inverse_of(final, scales):

time: 82.3 us -> 81.9 us (level)
  no operation moved by 1% of the time
where the time goes in v5:
time: 81.9 us; the launch traced here: 81.7 us
  Pallas kernels  80 us (98%)
  local copies, waits for them, and re-layouts  1.04 us (1%)
    pallas_call x1, Pallas kernels, exchange(): pl.pallas_call(functools.partial(exchange_kernel, sizes), out_shape=(jax....  58.2 us
    pallas_call x1, Pallas kernels, factor(): pl.pallas_call(factor_kernel, out_shape=(jax.ShapeDtypeStruct((rows, rows...  19.9 us
    pallas_call x1, Pallas kernels, arrange(): pl.pallas_call(arrange_kernel, out_shape=jax.ShapeDtypeStruct((fibers, ro...  1.89 us

profile of v5, /device:TPU:1, one launch (start us, length us, event | category | flops | bytes accessed | tf_op | source)
XLA Modules:
  0.0 81.7 jit_solution(4000441098143659776)
XLA Ops:
  0.6 1.9 %shard_map.58.outgoing = bf16[16,32,512]{2,1,0:T(8,128)(2,1)} custom-call(s32[1,1,16]{2,1,0:T(1,128)} %owner_ref.1, bf16[32,8192]{1,0:T(8,128)(2,1)} %slab_ref.1), custom_call_target="tpu_custom_call" | custom-call | tf_op jit(solution)/shard_map/pallas_call | solution.py:215
  2.5 0.0 copy-start
  2.5 1.0 %copy-done = bf16[16,32,512]{2,1,0:T(8,128)(2,1)S(1)} copy-done((bf16[16,32,512]{2,1,0:T(8,128)(2,1)S(1)}, bf16[16,32,512]{2,1,0:T(8,128)(2,1)}, u32[]{:S(2)}) %copy-start) | copy-done | bytes 524312
  3.6 0.0 copy-start.1
  3.6 58.2 %shard_map.59 = (bf16[512,512]{1,0:T(8,128)(2,1)S(1)}, f32[2,4,8,24,128]{4,3,2,1,0:T(8,128)S(1)}) custom-call(bf16[16,32,512]{2,1,0:T(8,128)(2,1)S(1)} %copy-done), custom_call_target="tpu_custom_call" | custom-call | tf_op jit(solution)/shard_map/pallas_call | solution.py:239
  61.7 0.0 copy-done.1
  61.8 19.9 %shard_map.60 = (f32[512,512]{1,0:T(8,128)}, f32[512,128]{1,0:T(8,128)}, bf16[128,512]{1,0:T(8,128)(2,1)}) custom-call(f32[2,4,8,24,128]{4,3,2,1,0:T(8,128)S(1)} %get-tuple-element.5.pieces_ref, f32[512,128]{1,0:T(8,128)S(1)} %copy-done.1, bf16[512,512]{1,0:T(8,128)(2,1)S(1)} %get-tuple-element.6.columns_ref), custom_call_target="tpu_custom_call" | custom-call | tf_op jit(solution)/shard_map/pallas_call | solution.py:450
Async XLA Ops:
  2.5 1.0 %copy-start = (bf16[16,32,512]{2,1,0:T(8,128)(2,1)S(1)}, bf16[16,32,512]{2,1,0:T(8,128)(2,1)}, u32[]{:S(2)}) copy-start(bf16[16,32,512]{2,1,0:T(8,128)(2,1)} %shard_map.58.outgoing) | copy-start | bytes 1572868
  3.6 58.2 %copy-start.1 = (f32[512,128]{1,0:T(8,128)S(1)}, f32[512,128]{1,0:T(8,128)}, u32[]{:S(2)}) copy-start(f32[512,128]{1,0:T(8,128)} %start_ref.1) | copy-start | bytes 786436

commit v6 on v4

--- a/solution.py
+++ b/solution.py
@@ -165,7 +165,7 @@
     for place in range(y_size - 1, 0, -1):
         target = {"gz": (y + near[place - 1]) % y_size}
         send((core, x, 0), (core, x, place), y_sems, place - 1, target)
-    groups = [pl.ds(0, y_size // 2), pl.ds(y_size // 2, y_size // 2)]
+    groups = [pl.ds(0, y_size)]
     x_steps = sorted(range(1, x_size), key=lambda step: min(step, x_size - step))
     for number, group in enumerate(groups):
         for place in range(max(group.start, 1), group.start + group.size):

time: 82.3 us -> 82.8 us (level)
  no operation moved by 1% of the time
where the time goes in v6:
time: 82.8 us; the launch traced here: 82.6 us
  Pallas kernels  80.9 us (98%)
  local copies, waits for them, and re-layouts  1.04 us (1%)
    pallas_call x1, Pallas kernels, exchange(): pl.pallas_call(functools.partial(exchange_kernel, sizes), out_shape=(jax....  58.7 us
    pallas_call x1, Pallas kernels, factor(): pl.pallas_call(factor_kernel, out_shape=(jax.ShapeDtypeStruct((rows, rows...  20.3 us
    pallas_call x1, Pallas kernels, arrange(): pl.pallas_call(arrange_kernel, out_shape=jax.ShapeDtypeStruct((fibers, ro...  1.89 us

profile of v6, /device:TPU:1, one launch (start us, length us, event | category | flops | bytes accessed | tf_op | source)
XLA Modules:
  0.0 82.6 jit_solution(3770249028705775761)
XLA Ops:
  0.6 1.9 %shard_map.58.outgoing = bf16[16,32,512]{2,1,0:T(8,128)(2,1)} custom-call(s32[1,1,16]{2,1,0:T(1,128)} %owner_ref.1, bf16[32,8192]{1,0:T(8,128)(2,1)} %slab_ref.1), custom_call_target="tpu_custom_call" | custom-call | tf_op jit(solution)/shard_map/pallas_call | solution.py:215
  2.5 0.0 copy-start
  2.5 1.0 %copy-done = bf16[16,32,512]{2,1,0:T(8,128)(2,1)S(1)} copy-done((bf16[16,32,512]{2,1,0:T(8,128)(2,1)S(1)}, bf16[16,32,512]{2,1,0:T(8,128)(2,1)}, u32[]{:S(2)}) %copy-start) | copy-done | bytes 524312
  3.6 0.0 copy-start.1
  3.6 58.7 %shard_map.59 = (bf16[512,512]{1,0:T(8,128)(2,1)S(1)}, f32[2,4,8,24,128]{4,3,2,1,0:T(8,128)S(1)}) custom-call(bf16[16,32,512]{2,1,0:T(8,128)(2,1)S(1)} %copy-done), custom_call_target="tpu_custom_call" | custom-call | tf_op jit(solution)/shard_map/pallas_call | solution.py:239
  62.3 0.0 copy-done.1
  62.3 20.3 %shard_map.60 = (f32[512,512]{1,0:T(8,128)}, f32[512,128]{1,0:T(8,128)}, bf16[128,512]{1,0:T(8,128)(2,1)}) custom-call(f32[2,4,8,24,128]{4,3,2,1,0:T(8,128)S(1)} %get-tuple-element.5.pieces_ref, f32[512,128]{1,0:T(8,128)S(1)} %copy-done.1, bf16[512,512]{1,0:T(8,128)(2,1)S(1)} %get-tuple-element.6.columns_ref), custom_call_target="tpu_custom_call" | custom-call | tf_op jit(solution)/shard_map/pallas_call | solution.py:450
Async XLA Ops:
  2.5 1.0 %copy-start = (bf16[16,32,512]{2,1,0:T(8,128)(2,1)S(1)}, bf16[16,32,512]{2,1,0:T(8,128)(2,1)}, u32[]{:S(2)}) copy-start(bf16[16,32,512]{2,1,0:T(8,128)(2,1)} %shard_map.58.outgoing) | copy-start | bytes 1572868
  3.6 58.7 %copy-start.1 = (f32[512,128]{1,0:T(8,128)S(1)}, f32[512,128]{1,0:T(8,128)}, u32[]{:S(2)}) copy-start(f32[512,128]{1,0:T(8,128)} %start_ref.1) | copy-start | bytes 786436
